TPU v7x, 32 devices: a whole 2x2x4 slice. The times are simulated.
32 devices in a mesh: grp: 4 (over y, core), dev: 8 (over z, x).
Axes of the slice: x: 2, y: 2, z: 4, core: 2. Of those that a mesh axis runs over, the one named last changes fastest.
Arguments:
- matrix: float32 [16384, 128], P(('grp', 'dev')), may hold values from -6 to 6
- flip_bits: int32 [16384], P(('grp', 'dev')), may hold values from 0 to 1
- sample_rows: int32 [2048], replicated, may hold values from 0 to 16383
Outputs:
- sketch: float32 [2048, 128], P(('grp', 'dev'))
- gram: float32 [128, 128], replicated
Inputs may be any that keep to these rules, and one draw needn't show every extreme that they name: `sample_rows`: rows may repeat.
All inputs are finite; a program needn't handle non-finite values.
Results may differ from a plain program's by a relative error of at most 0.000098.
Values sent between devices are 32-bit elements; how exact they have to be, the bound alone decides.
A program may use at most 64 MiB of HBM per device.

v0:
```python
import jax
import jax.numpy as jnp
from jax import lax
from jax.sharding import PartitionSpec as P


def hadamard_table(order):
    rows_idx = lax.broadcasted_iota(jnp.int32, (order, order), 0)
    cols_idx = lax.broadcasted_iota(jnp.int32, (order, order), 1)
    common = rows_idx & cols_idx
    parity = jnp.zeros((order, order), jnp.int32)
    for level in range(order.bit_length() - 1):
        parity = parity ^ common >> level & 1
    return (1 - 2 * parity).astype(jnp.float32)


def body(matrix, flip_bits, sample_rows):
    rows_dev, width = matrix.shape
    log_rows = rows_dev.bit_length() - 1
    outer = 2 ** (log_rows // 2)
    inner = rows_dev // outer
    n_inner = lax.axis_size("dev")
    n_outer = lax.axis_size("grp")
    devices = n_inner * n_outer
    my_index = lax.axis_index("grp") * n_inner + lax.axis_index("dev")
    signs = (1 - 2 * flip_bits).astype(jnp.float32)
    cube = (matrix * signs[:, None]).reshape(outer, inner, width)
    cube = jnp.einsum("ia,ajf->ijf", hadamard_table(outer), cube, precision=lax.Precision.HIGHEST)
    cube = jnp.einsum("jb,ibf->ijf", hadamard_table(inner), cube, precision=lax.Precision.HIGHEST)
    field = cube.reshape(rows_dev, width)
    pending = devices - 1
    keep_mask = devices - 1 ^ pending
    scale = 1.0 / jnp.sqrt(jnp.float32(rows_dev * devices))
    total_bits = devices.bit_length() - 1
    owner = sample_rows // rows_dev
    local_row = sample_rows % rows_dev
    picked = jnp.take(field, local_row, axis=0)
    common = owner & my_index & pending
    parity = jnp.zeros_like(common)
    for level in range(total_bits):
        parity = parity ^ common >> level & 1
    same = (owner ^ my_index) & keep_mask == 0
    weight = jnp.where(same, (1 - 2 * parity).astype(jnp.float32), jnp.float32(0.0)) * scale
    sketch = lax.psum_scatter(
        picked * weight[:, None], ("grp", "dev"), scatter_dimension=0, tiled=True
    )
    partial_gram = jnp.dot(
        sketch.T, sketch, preferred_element_type=jnp.float32, precision=lax.Precision.HIGHEST
    )
    gram = lax.psum(partial_gram, ("grp", "dev")) / sample_rows.shape[0]
    return (sketch, gram)


def solution(mesh):
    return jax.shard_map(
        body,
        mesh=mesh,
        in_specs=(P(("grp", "dev"), None), P(("grp", "dev")), P()),
        out_specs=(P(("grp", "dev"), None), P()),
        check_vma=False,
    )
```

profile of v0, /device:TPU:1, one launch (start us, length us, event | category | flops | bytes accessed | tf_op | source)
XLA Modules:
  0.0 288.8 jit_solution(661740037963289966)
XLA Ops:
  7.2 0.0 reduce-scatter.2.cloned.1.call-start
  7.2 0.0 copy-start
  7.2 0.8 broadcast_clamp_fusion
  8.0 0.0 copy-done
  8.0 0.0 copy-start.1
  8.0 0.7 copy-done.1
  8.7 1.1 broadcast_multiply_fusion
  9.8 0.5 fusion.2
  10.3 0.4 fusion
  10.7 5.5 %gather_fusion = f32[2048,128]{1,0:T(8,128)S(1)} fusion(f32[512,128]{1,0:T(8,128)S(1)} %bitcast.12, s32[2048]{0:T(1024)S(1)} %broadcast_clamp_fusion), kind=kCustom, calls=%fused_computation | custom fusion | bytes 2105344 | tf_op jit(solution)/shard_map/jit(_take)/gather | solution.py:37
  16.2 1.5 select_multiply_fusion
  17.7 0.0 reduce-scatter.2.cloned.1.call-update
  17.7 0.0 all-reduce.2.cloned.1.call-start
  17.8 130.9 %reduce-scatter.2.cloned.1.call-done = f32[64,128]{1,0:T(8,128)} async-done(((f32[2048,128]{1,0:T(8,128)}), f32[64,128]{1,0:T(8,128)}) %reduce-scatter.2.cloned.1.call-update) | async-done | bytes 32784 | tf_op jit(solution)/shard_map/reduce_scatter | solution.py:44
  148.7 1.8 fusion.65
  150.4 0.0 all-reduce.2.cloned.1.call-update
  150.4 130.0 %all-reduce.2.cloned.1.call-done = f32[128,128]{1,0:T(8,128)} async-done(((f32[128,128]{1,0:T(8,128)}), f32[128,128]{1,0:T(8,128)}) %all-reduce.2.cloned.1.call-update) | async-done | bytes 65552 | tf_op jit(solution)/shard_map/psum | solution.py:50
  280.5 1.5 broadcast_multiply_fusion.1
  (3 shorter events, 0.0 us)
Async XLA Ops:
  7.2 141.5 %reduce-scatter.2.cloned.1.call-start = ((), (), s32[]{:S(2)}) async-start(), calls=%async_computation.1 | async-start | bytes 1081344 | tf_op jit(solution)/shard_map/reduce_scatter | solution.py:44
  7.2 0.8 copy-start
  8.0 0.7 copy-start.1
  17.7 262.7 %all-reduce.2.cloned.1.call-start = ((), (), s32[]{:S(2)}) async-start(), calls=%async_computation.2 | async-start | bytes 131072 | tf_op jit(solution)/shard_map/psum | solution.py:50
Sparse Core Ops, SparseCore 0:
  17.9 130.7 reduce-scatter.1
  154.8 125.5 all-reduce.1
where the time goes:
time: 289 us
  waiting for transfers between devices  261 us (90%)
  between operations  14.1 us (5%)
  local copies, waits for them, and re-layouts  6.13 us (2%)
  other arithmetic  4.86 us (2%)
    reduce_scatter x1, waiting for transfers between devices, body(): lax.psum_scatter(picked * weight[:, None], ('grp', 'dev'), scatter_dimens...  131 us
    psum x1, waiting for transfers between devices, body(): gram = lax.psum(partial_gram, ('grp', 'dev')) / sample_rows.shape[0]  130 us
  transfers between devices with their start and end apart: 2, of which 2 were waited for; matrix products, arithmetic and copies ran while one was open for 0% of the time, Pallas kernels for 0%

commit v1 on v0

--- a/solution.py
+++ b/solution.py
@@ -47,7 +47,7 @@
     partial_gram = jnp.dot(
         sketch.T, sketch, preferred_element_type=jnp.float32, precision=lax.Precision.HIGHEST
     )
-    gram = lax.psum(partial_gram, ("grp", "dev")) / sample_rows.shape[0]
+    gram = jnp.sum(lax.all_gather(partial_gram, ("grp", "dev")), axis=0) / sample_rows.shape[0]
     return (sketch, gram)
 
 

time: 289 us -> 225 us (0.78)
  waiting for transfers between devices: 261 us -> 194 us
  other arithmetic: 4.86 us -> 7.76 us
    psum x1 -> x0, waiting for transfers between devices: 130 us -> none  [body(): gram = lax.psum(partial_gram, ('grp', 'dev')) / sample_rows.shape[0]]
    all_gather x0 -> x1, waiting for transfers between devices: none -> 62.8 us  [body(): lax.all_gather(partial_gram, ('grp', 'dev'))]
where the time goes in v1:
time: 225 us; the launch traced here: 224 us
  waiting for transfers between devices  194 us (86%)
  between operations  14.1 us (6%)
  other arithmetic  7.76 us (3%)
  local copies, waits for them, and re-layouts  5.47 us (2%)
  matrix products  2.67 us (1%)
    reduce_scatter x1, waiting for transfers between devices, body(): lax.psum_scatter(picked * weight[:, None], ('grp', 'dev'), scatter_dimens...  131 us
    all_gather x1, waiting for transfers between devices, body(): lax.all_gather(partial_gram, ('grp', 'dev'))  62.8 us
    gather x1, local copies, waits for them, and re-layouts, body(): picked = jnp.take(field, local_row, axis=0)  5.47 us
  transfers between devices with their start and end apart: 2, of which 2 were waited for; matrix products, arithmetic and copies ran while one was open for 0% of the time, Pallas kernels for 0%

profile of v1, /device:TPU:1, one launch (start us, length us, event | category | flops | bytes accessed | tf_op | source)
XLA Modules:
  0.0 224.0 jit_solution(9916513564506491391)
XLA Ops:
  7.2 0.0 reduce-scatter.2.cloned.1.call-start
  7.2 0.7 compare_and_fusion
  7.9 0.7 broadcast_clamp_fusion
  8.6 0.7 subtract_convert_fusion
  9.3 0.7 convert_multiply_fusion
  10.1 1.1 broadcast_multiply_fusion
  11.1 0.5 fusion.2
  11.6 0.4 fusion
  12.1 5.5 %gather_fusion = f32[2048,128]{1,0:T(8,128)S(1)} fusion(f32[512,128]{1,0:T(8,128)S(1)} %bitcast.13, s32[2048]{0:T(1024)S(1)} %broadcast_clamp_fusion), kind=kCustom, calls=%fused_computation | custom fusion | bytes 2105344 | tf_op jit(solution)/shard_map/jit(_take)/gather | solution.py:37
  17.6 1.5 select_multiply_fusion
  19.1 0.0 reduce-scatter.2.cloned.1.call-update
  19.1 0.0 all-gather.3.cloned.1.call-start
  19.1 131.0 %reduce-scatter.2.cloned.1.call-done = f32[64,128]{1,0:T(8,128)} async-done(((f32[2048,128]{1,0:T(8,128)}), f32[64,128]{1,0:T(8,128)}) %reduce-scatter.2.cloned.1.call-update) | async-done | bytes 32784 | tf_op jit(solution)/shard_map/reduce_scatter | solution.py:44
  150.2 1.8 fusion.65
  151.9 0.0 all-gather.3.cloned.1.call-update
  152.0 62.8 %all-gather.3.cloned.1.call-done = f32[4096,128]{1,0:T(8,128)} async-done(((f32[128,128]{1,0:T(8,128)}), f32[4096,128]{1,0:T(8,128)}) %all-gather.3.cloned.1.call-update) | async-done | bytes 2097168 | tf_op jit(solution)/shard_map/all_gather | solution.py:50
  214.8 1.7 reduce_sum.9
  216.5 0.6 broadcast_multiply_fusion.1
Async XLA Ops:
  7.2 143.0 %reduce-scatter.2.cloned.1.call-start = ((), (), s32[]{:S(2)}) async-start(), calls=%async_computation.1 | async-start | bytes 1081344 | tf_op jit(solution)/shard_map/reduce_scatter | solution.py:44
  19.1 195.7 %all-gather.3.cloned.1.call-start = ((), (), s32[]{:S(2)}) async-start(), calls=%async_computation.2 | async-start | bytes 2162688 | tf_op jit(solution)/shard_map/all_gather | solution.py:50
Sparse Core Ops, SparseCore 0:
  19.2 130.9 reduce-scatter.1
  153.7 61.0 all-gather.2
